TPU v7x, 32 devices: a whole 2x2x4 slice. The times are simulated.
32 devices in a mesh: bucket: 16 (over z, y, x), seq: 2 (over core).
Axes of the slice: x: 2, y: 2, z: 4, core: 2. Of those that a mesh axis runs over, the one named last changes fastest.
Arguments:
- tokens: bfloat16 [64, 512, 384], P('bucket', 'seq'), may hold values from -6 to 6
- cotangent: bfloat16 [64, 512, 384], P('bucket', 'seq'), may hold values from -6 to 6
- segment_ids: int32 [64, 512], P('bucket'), may hold values from 0 to 7, never falling along the last dimension, each value on 1 to 256 neighbouring positions
- pad_counts: int32 [64], P('bucket'), may hold values from 0 to 128
- timesteps: int32 [64, 8], P('bucket'), may hold values from 0 to 999
- classes: int32 [64, 8], P('bucket'), may hold values from 0 to 999
- head_mask: int32 [64, 8, 6], P('bucket'), may hold values 0 or 1
- channel_mask: int32 [64, 8, 24], P('bucket'), may hold values 0 or 1
- keep_mask: int32 [64, 512], P('bucket', 'seq'), may hold values 0 or 1
- class_table: bfloat16 [1000, 384], replicated, may hold values from -6 to 6
- w_ada: bfloat16 [384, 2304], P('bucket', 'seq'), may hold values from -0.3125 to 0.3125
- b_ada: bfloat16 [2304], P('seq'), may hold values from -2 to 2
- w_qkv: bfloat16 [384, 1152], replicated, may hold values from -0.3125 to 0.3125
- bias_qv: bfloat16 [768], replicated, may hold values from -2 to 2
- w_proj: bfloat16 [384, 384], replicated, may hold values from -2.5 to 2.5
- b_proj: bfloat16 [384], replicated, may hold values from -2 to 2
- w_fc1: bfloat16 [384, 1536], replicated, may hold values from -0.3125 to 0.3125
- b_fc1: bfloat16 [1536], replicated, may hold values from -2 to 2
- w_fc2: bfloat16 [1536, 384], replicated, may hold values from -0.15625 to 0.15625
- b_fc2: bfloat16 [384], replicated, may hold values from -2 to 2
- w_router: bfloat16 [384], replicated, may hold values from -0.3125 to 0.3125
Outputs:
- output: bfloat16 [64, 512, 384], P('bucket', 'seq')
- grad_tokens: bfloat16 [64, 512, 384], P('bucket', 'seq')
- grad_class_table: float32 [1000, 384], P(None, 'bucket')
- grad_w_ada: float32 [384, 2304], P('bucket', 'seq')
- grad_b_ada: float32 [2, 1152], P('seq', 'bucket')
- grad_w_qkv: float32 [384, 1152], P(None, 'bucket')
- grad_bias_qv: float32 [768], P('bucket')
- grad_w_proj: float32 [384, 384], P(None, 'bucket')
- grad_b_proj: float32 [384], P('bucket')
- grad_w_fc1: float32 [384, 1536], P(None, 'bucket')
- grad_b_fc1: float32 [1536], P('bucket')
- grad_w_fc2: float32 [1536, 384], P('bucket')
- grad_b_fc2: float32 [384], P('bucket')
- grad_w_router: float32 [384], P('bucket')
Inputs may be any that keep to these rules, and one draw needn't show every extreme that they name: `segment_ids`: crop numbers never fall along a row; each crop has 1 to 256 tokens and one has exactly 256. The padding tokens are the last pad_counts[r] tokens of row r.
All inputs are finite; a program needn't handle non-finite values. No bound on the sum of `head_mask` or of `channel_mask` or of `keep_mask` on one device may be relied on, other than what follows from the above.
Results may differ from a plain program's by a relative error of at most 0.014.
The roundings to bfloat16 on the way count: a program that leaves them out, or rounds other values in their place, can miss the bound.
Values may be sent and summed in bfloat16 or wider, within the bound.
No kernel may reach another device: no remote copies, remote signals or barrier semaphores. Data moves between devices by JAX's collectives and lax.ppermute only.
A program may use at most 192 MiB of HBM per device.

v0:
```python
from functools import partial
import math
import jax
import jax.numpy as jnp
from jax import lax
from jax.sharding import PartitionSpec as P

D = 384
HEADS = 6
HEAD_DIM = 64
FF = 1536
NCLASS = 1000
CGROUPS = 24
CROPS = 8
HIGHEST_PRECISION = lax.Precision.HIGHEST
EPSILON = 1e-06
NEGATIVE = -1e30


def exact(form, left, right):
    return jnp.einsum(form, left, right, precision=HIGHEST_PRECISION)


def layer_norm(values_in):
    centred = values_in - jnp.mean(values_in, -1, keepdims=True)
    variance = jnp.mean(centred * centred, -1, keepdims=True)
    return centred * lax.rsqrt(variance + EPSILON)


def time_embed(timesteps):
    half_width = D // 2
    frequency = jnp.exp(-math.log(10000.0) * jnp.arange(half_width, dtype=jnp.float32) / half_width)
    angles = timesteps.astype(jnp.float32)[..., None] * frequency
    return jnp.concatenate([jnp.cos(angles), jnp.sin(angles)], -1)


def first_norm(token_in, shift_in, scale_in):
    return layer_norm(token_in) * (1.0 + scale_in) + shift_in


def heads_view(matrix):
    return matrix.reshape(matrix.shape[0], HEADS, HEAD_DIM)


def body(
    tokens,
    cotangent,
    segment_ids,
    pad_counts,
    timesteps,
    classes,
    head_mask,
    channel_mask,
    keep_mask,
    class_table,
    w_ada,
    b_ada,
    w_qkv,
    bias_qv,
    w_proj,
    b_proj,
    w_fc1,
    b_fc1,
    w_fc2,
    b_fc2,
    w_router,
):
    row_count, local_len, width_all = tokens.shape
    full_len = local_len * lax.axis_size("seq")
    first_pos = lax.axis_index("seq") * local_len
    token_count = row_count * local_len
    shape_three = (row_count, local_len, D)
    position = jnp.arange(full_len, dtype=jnp.int32)
    live_row = position[None, :] < (full_len - pad_counts)[:, None]
    attend_keys = jnp.where(live_row, segment_ids, -1)
    attend_query = lax.dynamic_slice_in_dim(attend_keys, first_pos, local_len, 1)
    live_here = lax.dynamic_slice_in_dim(live_row.astype(jnp.float32), first_pos, local_len, 1)
    crop_here = lax.dynamic_slice_in_dim(segment_ids, first_pos, local_len, 1)
    crop_hot = (crop_here[:, :, None] == jnp.arange(CROPS, dtype=jnp.int32)).astype(jnp.float32)
    class_hot = (classes[:, :, None] == jnp.arange(NCLASS, dtype=jnp.int32)).astype(jnp.float32)
    ada_full = lax.all_gather(w_ada, "bucket", axis=0, tiled=True)
    condition = time_embed(timesteps) + exact(
        "rcn,nd->rcd", class_hot, class_table.astype(jnp.float32)
    )
    silu_value, pull_silu = jax.vjp(jax.nn.silu, condition)
    silu_low = silu_value.astype(jnp.bfloat16)
    mod_part = jnp.einsum(
        "rcd,dm->rcm", silu_low, ada_full, preferred_element_type=jnp.float32
    ) + b_ada.astype(jnp.float32)
    modulation = lax.all_gather(mod_part, "seq", axis=2, tiled=True)
    per_token = exact("rlc,rcm->rlm", crop_hot, modulation)
    shift_one, scale_one, gate_one, shift_two, scale_two, gate_two = jnp.split(
        per_token, 6, axis=-1
    )
    token_float = tokens.astype(jnp.float32)
    hidden_one, pull_first = jax.vjp(first_norm, token_float, shift_one, scale_one)
    hidden_low = hidden_one.astype(jnp.bfloat16).reshape(token_count, D)
    projected = jnp.dot(hidden_low, w_qkv, preferred_element_type=jnp.float32)
    bias_float = bias_qv.astype(jnp.float32)
    query = (projected[:, :D] + bias_float[:D]).astype(jnp.bfloat16).reshape(shape_three)
    key_here = projected[:, D : 2 * D].astype(jnp.bfloat16).reshape(shape_three)
    value_here = (projected[:, 2 * D :] + bias_float[D:]).astype(jnp.bfloat16).reshape(shape_three)
    key_rows, value_rows = (
        lax.all_gather(key_here, "seq", axis=1, tiled=True),
        lax.all_gather(value_here, "seq", axis=1, tiled=True),
    )
    same_crop = attend_query[:, :, None] == attend_keys[:, None, :]
    score_scale = HEAD_DIM ** (-0.5)

    def raw_scores(query_row, key_row, same_row):
        scores = (
            jnp.einsum(
                "qhe,khe->hqk",
                heads_view(query_row),
                heads_view(key_row),
                preferred_element_type=jnp.float32,
            )
            * score_scale
        )
        return jnp.where(same_row[None], scores, NEGATIVE)

    def attend(item):
        query_row, key_row, value_row, same_row = item
        scores = raw_scores(query_row, key_row, same_row)
        row_max = jnp.max(scores, -1, keepdims=True)
        numerator = jnp.exp(scores - row_max)
        denominator = jnp.sum(numerator, -1, keepdims=True)
        probability = (numerator / denominator).astype(jnp.bfloat16)
        mixed_heads = jnp.einsum(
            "hqk,khe->qhe", probability, heads_view(value_row), preferred_element_type=jnp.float32
        )
        return (mixed_heads, (row_max + jnp.log(denominator))[..., 0])

    mixed_heads, log_total = lax.map(attend, (query, key_rows, value_rows, same_crop))
    head_scale = exact("rlc,rch->rlh", crop_hot, head_mask.astype(jnp.float32))[..., None]
    attended = (mixed_heads * head_scale).astype(jnp.bfloat16).reshape(token_count, D)
    branch = (
        jnp.dot(attended, w_proj, preferred_element_type=jnp.float32) + b_proj.astype(jnp.float32)
    ).reshape(shape_three)
    live_column = live_here[..., None]

    def second_norm(token_in, branch_in, gate_in, shift_in, scale_in):
        residual_in = token_in + live_column * gate_in * branch_in
        return (residual_in, layer_norm(residual_in) * (1.0 + scale_in) + shift_in)

    (residual, hidden_two), pull_second = jax.vjp(
        second_norm, token_float, branch, gate_one, shift_two, scale_two
    )
    second_low = hidden_two.astype(jnp.bfloat16).reshape(token_count, D)
    router_rate = jax.nn.sigmoid(jnp.dot(second_low, w_router, preferred_element_type=jnp.float32))
    pre_act = jnp.dot(second_low, w_fc1, preferred_element_type=jnp.float32) + b_fc1.astype(
        jnp.float32
    )
    chans_tok = exact(
        "rlc,rcf->rlf",
        crop_hot,
        jnp.repeat(channel_mask.astype(jnp.float32), FF // CGROUPS, axis=-1),
    ).reshape(token_count, FF)
    gelu_out, pull_gelu = jax.vjp(partial(jax.nn.gelu, approximate=True), pre_act)
    activation = (gelu_out * chans_tok).astype(jnp.bfloat16)
    mlp_out = jnp.dot(activation, w_fc2, preferred_element_type=jnp.float32) + b_fc2.astype(
        jnp.float32
    )
    keep_live = (live_here * keep_mask.astype(jnp.float32)).reshape(token_count)
    branch_coef = keep_live * router_rate
    gate_flat = gate_two.reshape(token_count, D)
    outcome = residual.reshape(token_count, D) + branch_coef[:, None] * gate_flat * mlp_out
    output = outcome.astype(jnp.bfloat16).reshape(shape_three)
    grad_out = cotangent.astype(jnp.float32).reshape(token_count, D)
    grad_mlp = (grad_out * branch_coef[:, None] * gate_flat).astype(jnp.bfloat16)
    grad_gate_two = grad_out * branch_coef[:, None] * mlp_out
    grad_rate = jnp.sum(grad_out * gate_flat * mlp_out, -1) * keep_live
    grad_logit = grad_rate * router_rate * (1.0 - router_rate)
    grad_w_fc2 = jnp.einsum("nf,nd->fd", activation, grad_mlp, preferred_element_type=jnp.float32)
    grad_b_fc2 = jnp.sum(grad_mlp.astype(jnp.float32), 0)
    grad_act = jnp.einsum("nd,fd->nf", grad_mlp, w_fc2, preferred_element_type=jnp.float32)
    grad_pre = pull_gelu(grad_act * chans_tok)[0].astype(jnp.bfloat16)
    grad_w_fc1 = jnp.einsum("nd,nf->df", second_low, grad_pre, preferred_element_type=jnp.float32)
    grad_b_fc1 = jnp.sum(grad_pre.astype(jnp.float32), 0)
    grad_w_router = exact("nd,n->d", second_low.astype(jnp.float32), grad_logit)
    grad_hidden_two = (
        jnp.einsum("nf,df->nd", grad_pre, w_fc1, preferred_element_type=jnp.float32)
        + grad_logit[:, None] * w_router.astype(jnp.float32)[None, :]
    )
    part_fc1, part_bfc1, part_fc2, part_bfc2, part_router = (
        lax.psum_scatter(grad_w_fc1, "bucket", scatter_dimension=1, tiled=True),
        lax.psum_scatter(grad_b_fc1, "bucket", scatter_dimension=0, tiled=True),
        lax.psum_scatter(grad_w_fc2, "bucket", scatter_dimension=0, tiled=True),
        lax.psum_scatter(grad_b_fc2, "bucket", scatter_dimension=0, tiled=True),
        lax.psum_scatter(grad_w_router, "bucket", scatter_dimension=0, tiled=True),
    )
    mlp_sums = (
        lax.psum(part_fc1.astype(jnp.bfloat16), "seq").astype(jnp.float32),
        lax.psum(part_bfc1.astype(jnp.bfloat16), "seq").astype(jnp.float32),
        lax.psum(part_fc2.astype(jnp.bfloat16), "seq").astype(jnp.float32),
        lax.psum(part_bfc2.astype(jnp.bfloat16), "seq").astype(jnp.float32),
        lax.psum(part_router.astype(jnp.bfloat16), "seq").astype(jnp.float32),
    )
    grad_token_one, grad_branch, grad_gate_one, grad_shift_two, grad_scale_two = pull_second(
        (grad_out.reshape(shape_three), grad_hidden_two.reshape(shape_three))
    )
    branch_low = grad_branch.astype(jnp.bfloat16).reshape(token_count, D)
    grad_w_proj = jnp.einsum("nd,ne->de", attended, branch_low, preferred_element_type=jnp.float32)
    grad_b_proj = jnp.sum(branch_low.astype(jnp.float32), 0)
    grad_attended = jnp.einsum(
        "ne,de->nd", branch_low, w_proj, preferred_element_type=jnp.float32
    ).astype(jnp.bfloat16)
    grad_heads = grad_attended.reshape(row_count, local_len, HEADS, HEAD_DIM) * head_scale.astype(
        jnp.bfloat16
    )

    def attend_back(item):
        query_row, key_row, value_row, same_row, total_row, grad_row = item
        scores = raw_scores(query_row, key_row, same_row)
        probability = jnp.exp(scores - total_row[..., None])
        grad_prob = jnp.einsum(
            "qhe,khe->hqk", grad_row, heads_view(value_row), preferred_element_type=jnp.float32
        )
        inner = jnp.sum(probability * grad_prob, -1)
        grad_scores = (probability * (grad_prob - inner[..., None])).astype(jnp.bfloat16)
        grad_query = (
            jnp.einsum(
                "hqk,khe->qhe", grad_scores, heads_view(key_row), preferred_element_type=jnp.float32
            )
            * score_scale
        ).astype(jnp.bfloat16)
        return (grad_query.reshape(-1, D), inner)

    grad_query, inner_total = lax.map(
        attend_back, (query, key_rows, value_rows, same_crop, log_total, grad_heads)
    )
    query_all, grad_heads_all = (
        lax.all_gather(query, "seq", axis=1, tiled=True),
        lax.all_gather(grad_heads, "seq", axis=1, tiled=True),
    )
    total_all, inner_all = (
        lax.all_gather(log_total, "seq", axis=2, tiled=True),
        lax.all_gather(inner_total, "seq", axis=2, tiled=True),
    )
    same_owner = attend_keys[:, :, None] == attend_query[:, None, :]

    def owner_back(item):
        query_row, key_row, value_row, same_row, total_row, inner_row, grad_row = item
        scores = raw_scores(query_row, key_row, same_row)
        probability = jnp.exp(scores - total_row[..., None])
        grad_prob = jnp.einsum(
            "qhe,khe->hqk", grad_row, heads_view(value_row), preferred_element_type=jnp.float32
        )
        grad_scores = (probability * (grad_prob - inner_row[..., None])).astype(jnp.bfloat16)
        grad_key = (
            jnp.einsum(
                "hqk,qhe->khe",
                grad_scores,
                heads_view(query_row),
                preferred_element_type=jnp.float32,
            )
            * score_scale
        ).astype(jnp.bfloat16)
        grad_value = jnp.einsum(
            "hqk,qhe->khe",
            probability.astype(jnp.bfloat16),
            grad_row,
            preferred_element_type=jnp.float32,
        ).astype(jnp.bfloat16)
        return (grad_key.reshape(-1, D), grad_value.reshape(-1, D))

    key_grad, value_grad = lax.map(
        owner_back,
        (query_all, key_here, value_here, same_owner, total_all, inner_all, grad_heads_all),
    )
    grad_projected = jnp.concatenate([grad_query, key_grad, value_grad], -1).reshape(
        token_count, 3 * D
    )
    grad_w_qkv = jnp.einsum(
        "nd,ne->de", hidden_low, grad_projected, preferred_element_type=jnp.float32
    )
    grad_bias_qv = jnp.concatenate(
        [
            jnp.sum(grad_projected[:, :D].astype(jnp.float32), 0),
            jnp.sum(grad_projected[:, 2 * D :].astype(jnp.float32), 0),
        ]
    )
    grad_hidden_one = jnp.einsum(
        "ne,de->nd", grad_projected, w_qkv, preferred_element_type=jnp.float32
    ).reshape(shape_three)
    grad_token_two, grad_shift_one, grad_scale_one = pull_first(grad_hidden_one)
    grad_tokens = (grad_token_one + grad_token_two).astype(jnp.bfloat16)
    grad_per_token = jnp.concatenate(
        [
            grad_shift_one,
            grad_scale_one,
            grad_gate_one,
            grad_shift_two,
            grad_scale_two,
            grad_gate_two.reshape(shape_three),
        ],
        -1,
    )
    mod_parts = exact("rlc,rlm->rcm", crop_hot, grad_per_token)
    grad_mod = lax.psum_scatter(
        mod_parts.astype(jnp.bfloat16), "seq", scatter_dimension=2, tiled=True
    )
    grad_w_ada = jnp.einsum("rcd,rcm->dm", silu_low, grad_mod, preferred_element_type=jnp.float32)
    grad_b_ada = jnp.sum(grad_mod.astype(jnp.float32), (0, 1))
    grad_silu = jnp.einsum("rcm,dm->rcd", grad_mod, ada_full, preferred_element_type=jnp.float32)
    grad_condition = pull_silu(grad_silu)[0]
    grad_table = exact("rcn,rcd->nd", class_hot, grad_condition)
    bucket_count = lax.axis_size("bucket")
    grad_w_ada, grad_b_ada = (
        lax.psum_scatter(grad_w_ada, "bucket", scatter_dimension=0, tiled=True),
        lax.psum_scatter(
            grad_b_ada.reshape(bucket_count, -1), "bucket", scatter_dimension=0, tiled=True
        ),
    )
    part_table, part_qkv, part_bias_qv, part_proj, part_bproj = (
        lax.psum_scatter(grad_table, "bucket", scatter_dimension=1, tiled=True),
        lax.psum_scatter(grad_w_qkv, "bucket", scatter_dimension=1, tiled=True),
        lax.psum_scatter(grad_bias_qv, "bucket", scatter_dimension=0, tiled=True),
        lax.psum_scatter(grad_w_proj, "bucket", scatter_dimension=1, tiled=True),
        lax.psum_scatter(grad_b_proj, "bucket", scatter_dimension=0, tiled=True),
    )
    attention_sums = (
        lax.psum(part_table.astype(jnp.bfloat16), "seq").astype(jnp.float32),
        lax.psum(part_qkv.astype(jnp.bfloat16), "seq").astype(jnp.float32),
        lax.psum(part_bias_qv.astype(jnp.bfloat16), "seq").astype(jnp.float32),
        lax.psum(part_proj.astype(jnp.bfloat16), "seq").astype(jnp.float32),
        lax.psum(part_bproj.astype(jnp.bfloat16), "seq").astype(jnp.float32),
    )
    summed = tuple(attention_sums) + tuple(mlp_sums)
    return (
        output,
        grad_tokens,
        summed[0],
        grad_w_ada,
        grad_b_ada,
        summed[1],
        summed[2],
        summed[3],
        summed[4],
        summed[5],
        summed[6],
        summed[7],
        summed[8],
        summed[9],
    )


def solution(mesh):
    placed = (
        P("bucket", "seq", None),
        P("bucket", "seq", None),
        P("bucket", None),
        P("bucket"),
        P("bucket", None),
        P("bucket", None),
        P("bucket", None, None),
        P("bucket", None, None),
        P("bucket", "seq"),
        P(),
        P("bucket", "seq"),
        P("seq"),
        P(),
        P(),
        P(),
        P(),
        P(),
        P(),
        P(),
        P(),
        P(),
    )
    return jax.shard_map(
        body,
        mesh=mesh,
        in_specs=placed,
        out_specs=(
            P("bucket", "seq", None),
            P("bucket", "seq", None),
            P(None, "bucket"),
            P("bucket", "seq"),
            P("seq", "bucket"),
            P(None, "bucket"),
            P("bucket"),
            P(None, "bucket"),
            P("bucket"),
            P(None, "bucket"),
            P("bucket"),
            P("bucket", None),
            P("bucket"),
            P("bucket"),
        ),
        check_vma=False,
    )
```

profile of v0, /device:TPU:0, one launch (start us, length us, event | category | flops | bytes accessed | tf_op | source)
XLA Modules:
  0.0 1123.7 jit_solution(7249561307434286096)
XLA Ops:
  8.0 48.0 %all_gather.24 = bf16[384,1152]{1,0:T(8,128)(2,1)S(1)} all-gather(bf16[24,1152]{1,0:T(8,128)(2,1)} %param.37), channel_id=1, replica_groups=mesh['bucket'=16,'seq'=2] {'bucket'}, dimensions={0}, use_global_device_ids=true | all-gather | bytes 940032 | tf_op jit(solution)/shard_map/all_gather | solution.py:81
  62.3 6.3 fusion.91
  90.9 4.5 fusion.89
  95.4 19.8 %while.36 = (s32[]{:T(128)}, f32[4,256,6,64]{1,3,2,0:T(8,128)}, f32[4,6,256]{2,1,0:T(8,128)S(1)}, bf16[4,512,384]{1,2,0:T(8,128)(2,1)}, pred[4,256,512]{2,1,0:T(...) while((s32[]{:T(128)}, f32[4,256,6,64]{1,3,2,0:T(8,128)}, ...), condition=%wide.region_5.6_spmd, body=%wide.region_2.5_spmd.sunk | while | flops 210762240 | bytes 13490789 | solution.py:134
  125.3 3.5 fusion.47
  128.9 3.6 fusion.69
  132.6 7.4 convert_reduce_fusion
  155.1 23.7 %while.37 = (s32[]{:T(128)}, bf16[4,256,384]{2,1,0:T(8,128)(2,1)S(1)}, f32[4,6,256]{2,1,0:T(8,128)S(1)}, bf16[4,512,384]{1,2,0:T(8,128)(2,1)}, pred[4,256,512]{2...) while((s32[]{:T(128)}, ...), condition=%wide.region_13.14_spmd, body=%wide.region_11.13_spmd.sunk | while | flops 310835712 | bytes 20830336 | solution.py:229
  189.2 64.5 %while.38 = (s32[]{:T(128)}, bf16[4,256,384]{2,1,0:T(8,128)(2,1)}, bf16[4,256,384]{2,1,0:T(8,128)(2,1)}, bf16[4,512,384]{1,2,0:T(8,128)(2,1)}, pred[4,512,256]{2...) while((s32[]{:T(128)}, bf16[4,256,384]{2,1,0:T(8,128)(2,1)}, ...), condition=%wide.region_15.16_spmd, body=%wide.region_14.15_spmd.sunk | while | flops 410812416 | bytes 16132277 | solution.py:267
  200.5 3.2 fusion.198
  248.6 3.2 fusion.198
  257.0 4.6 convert_reduce_fusion.2
  282.6 5.1 fusion.112
  288.9 5.1 fusion.111
  300.0 4.3 convolution_bitcast_fusion
  308.0 108.7 %reduce-scatter.28.cloned.1.call-done = f32[384,24]{0,1:T(8,128)} async-done(((f32[384,384]{0,1:T(8,128)}), f32[384,24]{0,1:T(8,128)}) %reduce-scatter.28.cloned.1.call-update) | async-done | bytes 36880
  419.8 129.3 %reduce-scatter.20.cloned.1.call-done = f32[96,384]{1,0:T(8,128)} async-done(((f32[1536,384]{1,0:T(8,128)}), f32[96,384]{1,0:T(8,128)}) %reduce-scatter.20.cloned.1.call-update) | async-done | bytes 147472 | tf_op jit(solution)/shard_map/reduce_scatter | solution.py:188
  550.6 131.7 %reduce-scatter.18.cloned.1.call-done = f32[384,96]{0,1:T(8,128)} async-done(((f32[384,1536]{0,1:T(8,128)}), f32[384,96]{0,1:T(8,128)}) %reduce-scatter.18.cloned.1.call-update) | async-done | bytes 147472 | tf_op jit(solution)/shard_map/reduce_scatter | solution.py:186
  684.1 75.1 %all-reduce.9 = (f32[16,72]{1,0:T(8,128)S(1)}, bf16[768]{0:T(1024)(128)(2,1)S(1)}, bf16[384]{0:T(512)(128)(2,1)S(1)}, bf16[1536]{0:T(1024)(128)(2,1)S(1)}, bf16[...) all-reduce(f32[16,72]{1,0:T(8,128)S(1)} %reshape.261, ...), channel_id=5, replica_groups=mesh['bucket'=16,'seq'=2] {'bucket'}, use_global_device_ids=true, to_apply=%region_23.24.clone | all-reduce | flops 4608 | bytes 29952
  762.2 48.7 %reduce-scatter.16.cloned.1.call-done = f32[1000,24]{0,1:T(8,128)} async-done(((f32[1000,384]{0,1:T(8,128)}), f32[1000,24]{0,1:T(8,128)}) %reduce-scatter.16.cloned.1.call-update) | async-done | bytes 96016 | tf_op jit(solution)/shard_map/reduce_scatter | solution.py:316
  812.4 128.9 %reduce-scatter.26.cloned.1.call-done = f32[384,72]{0,1:T(8,128)} async-done(((f32[384,1152]{0,1:T(8,128)}), f32[384,72]{0,1:T(8,128)}) %reduce-scatter.26.cloned.1.call-update) | async-done | bytes 110608
  945.7 15.5 %all-reduce.17.cloned.1.call-done = (bf16[384,96]{0,1:T(8,128)(2,1)}, bf16[96,384]{1,0:T(8,128)(2,1)}) async-done(((bf16[384,96]{0,1:T(8,128)(2,1)}, bf16[96,384]{1,0:T(8,128)(2,1)}), (bf16[384,96]{0,1:T(8,128)(2,1)}, bf16[96,384]{1,0:T(8,128)(2,1)})) %all-reduce.17.cloned.1.call-update) | async-done | bytes 147472 | tf_op jit(solution)/shard_map/psum | solution.py:193
  964.3 20.3 %all-reduce.15.cloned.1.call-done = (bf16[1000,24]{0,1:T(8,128)(2,1)}, bf16[384,72]{0,1:T(8,128)(2,1)}, bf16[48]{0:T(256)(128)(2,1)}, bf16[384,24]{0,1:T(8,128)(...) async-done(((bf16[1000,24]{0,1:T(8,128)(2,1)}, bf16[384,72]{0,1:T(8,128)(2,1)}, bf16[48]{0:T(256)(128)(2,1)}, ...) | async-done | bytes 122176 | tf_op jit(solution)/shard_map/psum | solution.py:323
  994.6 122.4 %reduce-scatter.24.cloned.1.call-done = f32[24,1152]{1,0:T(8,128)} async-done(((f32[384,1152]{1,0:T(8,128)}), f32[24,1152]{1,0:T(8,128)}) %reduce-scatter.24.cloned.1.call-update) | async-done | bytes 110608
  (423 shorter events, 226.1 us)
Async XLA Ops:
  7.2 118.1 %copy-start = (bf16[384,1536]{1,0:T(8,128)(2,1)S(1)}, bf16[384,1536]{1,0:T(8,128)(2,1)}, u32[]{:S(2)}) copy-start(bf16[384,1536]{1,0:T(8,128)(2,1)} %param.43) | copy-start | bytes 3538948
  7.2 88.2 %all-gather.5.cloned.1.call-start = ((), (), s32[]{:S(2)}) async-start(), calls=%async_computation.7 | async-start | bytes 2359296 | tf_op jit(solution)/shard_map/all_gather | solution.py:105
  8.0 52.9 %copy-start.6 = (bf16[4,256,384]{2,1,0:T(8,128)(2,1)S(1)}, bf16[4,256,384]{2,1,0:T(8,128)(2,1)}, u32[]{:S(2)}) copy-start(bf16[4,256,384]{2,1,0:T(8,128)(2,1)} %param.27) | copy-start | bytes 2359300
  62.3 28.6 %copy-start.39 = (s32[4,256]{1,0:T(4,128)}, s32[4,256]{1,0:T(4,128)S(1)}, u32[]{:S(2)}) copy-start(s32[4,256]{1,0:T(4,128)S(1)} %constant_dynamic-slice_fusion.10) | copy-start | bytes 12292
  76.3 19.2 %all-gather.7.cloned.1.call-start = ((), (), s32[]{:S(2)}) async-start(), calls=%async_computation.8 | async-start | bytes 2359296 | tf_op jit(solution)/shard_map/all_gather | solution.py:104
  79.0 105.3 %all-gather.11.cloned.1.call-start = ((), (), s32[]{:S(2)}) async-start(), calls=%async_computation.10 | async-start | bytes 2359296 | tf_op jit(solution)/shard_map/all_gather | solution.py:234
  89.7 57.0 %copy-start.47 = (f32[4,256]{1,0:T(4,128)}, f32[4,256]{1,0:T(4,128)S(1)}, u32[]{:S(2)}) copy-start(f32[4,256]{1,0:T(4,128)S(1)} %dynamic-slice_convert_fusion) | copy-start | bytes 12292
  121.4 23.1 %copy-start.2 = (f32[4,256,384]{2,1,0:T(8,128)}, f32[4,256,384]{2,1,0:T(8,128)S(1)}, u32[]{:S(2)}) copy-start(f32[4,256,384]{2,1,0:T(8,128)S(1)} %get-tuple-element.312) | copy-start | bytes 4718596
  121.4 23.1 %copy-start.35 = (f32[4,256]{1,0:T(4,128)}, f32[4,256]{1,0:T(4,128)S(1)}, u32[]{:S(2)}) copy-start(f32[4,256]{1,0:T(4,128)S(1)} %broadcast_multiply_fusion.1) | copy-start | bytes 12292
  121.8 22.7 %copy-start.41 = (f32[4,256]{1,0:T(4,128)}, f32[4,256]{1,0:T(4,128)S(1)}, u32[]{:S(2)}) copy-start(f32[4,256]{1,0:T(4,128)S(1)} %fusion.99) | copy-start | bytes 12292
  132.5 7.4 copy-start.69
  153.1 34.1 %all-gather.9.cloned.1.call-start = ((), (), s32[]{:S(2)}) async-start(), calls=%async_computation.9 | async-start | bytes 2359296 | tf_op jit(solution)/shard_map/all_gather | solution.py:233
  153.7 140.4 %reduce-scatter.22.cloned.1.call-start = ((), (), s32[]{:S(2)}) async-start(), calls=%async_computation.14 | async-start | bytes 884736
  279.6 137.1 %reduce-scatter.28.cloned.1.call-start = ((), (), s32[]{:S(2)}) async-start(), calls=%async_computation.17 | async-start | bytes 626688
  282.4 266.7 %reduce-scatter.20.cloned.1.call-start = ((), (), s32[]{:S(2)}) async-start(), calls=%async_computation.13 | async-start | bytes 2506752 | tf_op jit(solution)/shard_map/reduce_scatter | solution.py:188
  287.8 394.6 %reduce-scatter.18.cloned.1.call-start = ((), (), s32[]{:S(2)}) async-start(), calls=%async_computation.12 | async-start | bytes 2506752 | tf_op jit(solution)/shard_map/reduce_scatter | solution.py:186
  294.0 516.8 %reduce-scatter.16.cloned.1.call-start = ((), (), s32[]{:S(2)}) async-start(), calls=%async_computation.11 | async-start | bytes 1671168 | tf_op jit(solution)/shard_map/reduce_scatter | solution.py:316
  300.0 641.3 %reduce-scatter.26.cloned.1.call-start = ((), (), s32[]{:S(2)}) async-start(), calls=%async_computation.16 | async-start | bytes 1880064
  304.4 656.8 %all-reduce.17.cloned.1.call-start = ((), (), s32[]{:S(2)}) async-start(), calls=%async_computation.19 | async-start | bytes 294912 | tf_op jit(solution)/shard_map/psum | solution.py:193
  306.9 377.2 %copy-start.57 = (f32[384]{0:T(512)S(1)}, f32[384]{0:T(512)}, u32[]{:S(2)}) copy-start(f32[384]{0:T(512)} %get-tuple-element.309) | copy-start | bytes 4612
  306.9 377.2 %copy-start.59 = (f32[1536]{0:T(1024)S(1)}, f32[1536]{0:T(1024)}, u32[]{:S(2)}) copy-start(f32[1536]{0:T(1024)} %get-tuple-element.345) | copy-start | bytes 18436
  683.9 300.8 %all-reduce.15.cloned.1.call-start = ((), (), s32[]{:S(2)}) async-start(), calls=%async_computation.18 | async-start | bytes 250880 | tf_op jit(solution)/shard_map/psum | solution.py:323
  942.8 174.2 %reduce-scatter.24.cloned.1.call-start = ((), (), s32[]{:S(2)}) async-start(), calls=%async_computation.15 | async-start | bytes 1880064
  942.8 174.2 %copy-start.1 = (bf16[384,1536]{1,0:T(8,128)(2,1)S(1)}, bf16[384,1536]{1,0:T(8,128)(2,1)}, u32[]{:S(2)}) copy-start(bf16[384,1536]{1,0:T(8,128)(2,1)} %param.43) | copy-start | bytes 3538948
  (69 other events, 204.5 us)
Sparse Core Ops, SparseCore 0:
  76.4 5.6 all-gather.4
  83.6 10.8 all-gather.6
  153.2 9.8 all-gather.10
  164.5 10.8 all-gather.8
  279.8 8.2 reduce-scatter.21
  293.3 123.4 reduce-scatter.27
  421.7 127.3 reduce-scatter.19
  554.7 127.5 reduce-scatter.17
  687.1 123.7 reduce-scatter.15
  815.6 125.6 reduce-scatter.25
  944.2 16.9 all-reduce.16
  965.0 19.5 all-reduce.14
  990.1 126.8 reduce-scatter.23
where the time goes:
time: 1130 us; the launch traced here: 1120 us
  waiting for transfers between devices  706 us (62%)
  blocking collectives  129 us (11%)
  matrix products  112 us (10%)
  local copies, waits for them, and re-layouts  92.8 us (8%)
  other arithmetic  64.4 us (6%)
  between operations  17.1 us (2%)
    unnamed x17, waiting for transfers between devices  361 us
    reduce_scatter x1, waiting for transfers between devices, body(): lax.psum_scatter(grad_w_fc1, 'bucket', scatter_dimension=1, tiled=True)  132 us
    reduce_scatter x1, waiting for transfers between devices, body(): lax.psum_scatter(grad_w_fc2, 'bucket', scatter_dimension=0, tiled=True)  129 us
    unnamed x1, blocking collectives  75.1 us
    reduce_scatter x1, waiting for transfers between devices, body(): lax.psum_scatter(grad_table, 'bucket', scatter_dimension=1, tiled=True)  48.7 us
    all_gather x1, blocking collectives, body(): ada_full = lax.all_gather(w_ada, 'bucket', axis=0, tiled=True)  48 us
    unnamed x161, local copies, waits for them, and re-layouts  27.3 us
    dynamic_slice x24, local copies, waits for them, and re-layouts, body(): lax.map(attend, (query, key_rows, value_rows, same_crop))  24.4 us
  transfers between devices with their start and end apart: 13, of which 8 were waited for; matrix products, arithmetic and copies ran while one was open for 9% of the time, Pallas kernels for 0%

commit v1 on v0

--- a/solution.py
+++ b/solution.py
@@ -78,7 +78,16 @@
     crop_here = lax.dynamic_slice_in_dim(segment_ids, first_pos, local_len, 1)
     crop_hot = (crop_here[:, :, None] == jnp.arange(CROPS, dtype=jnp.int32)).astype(jnp.float32)
     class_hot = (classes[:, :, None] == jnp.arange(NCLASS, dtype=jnp.int32)).astype(jnp.float32)
-    ada_full = lax.all_gather(w_ada, "bucket", axis=0, tiled=True)
+    hold_thing_for = lambda xx, a_name, pos_dim: jnp.concatenate(
+        lax.all_to_all(
+            jnp.stack([xx] * lax.psum(1, axis_name=a_name)),
+            axis_name=a_name,
+            split_axis=0,
+            concat_axis=0,
+        ),
+        axis=pos_dim,
+    )
+    ada_full = hold_thing_for(w_ada, "bucket", 0)
     condition = time_embed(timesteps) + exact(
         "rcn,nd->rcd", class_hot, class_table.astype(jnp.float32)
     )

time: 1130 us -> 1110 us (0.982)
  blocking collectives: 129 us -> 81.1 us
  waiting for transfers between devices: 706 us -> 738 us
    all_gather x1 -> x0, blocking collectives: 48 us -> none  [body(): ada_full = lax.all_gather(w_ada, 'bucket', axis=0, tiled=True)]
    all_to_all x0 -> x1, waiting for transfers between devices: none -> 19.7 us  [body(): lax.all_to_all(jnp.stack([xx] * lax.psum(1, axis_name=a_name)), axis_name...]
    all_gather x1, waiting for transfers between devices: 0.01 us -> 11.8 us  [body(): lax.all_gather(key_here, 'seq', axis=1, tiled=True)]
    unnamed x161 -> x171, local copies, waits for them, and re-layouts: 27.3 us -> 25.6 us
  transfers between devices with their start and end apart: 13 -> 14, of which waited for: 8 -> 10; matrix products, arithmetic and copies ran while one was open for 9% -> 8% of each run, Pallas kernels for 0% -> 0%
where the time goes in v1:
time: 1110 us
  waiting for transfers between devices  738 us (66%)
  matrix products  111 us (10%)
  local copies, waits for them, and re-layouts  94.1 us (8%)
  blocking collectives  81.1 us (7%)
  other arithmetic  54.8 us (5%)
  between operations  17.4 us (2%)
    unnamed x17, waiting for transfers between devices  361 us
    reduce_scatter x1, waiting for transfers between devices, body(): lax.psum_scatter(grad_w_fc1, 'bucket', scatter_dimension=1, tiled=True)  132 us
    reduce_scatter x1, waiting for transfers between devices, body(): lax.psum_scatter(grad_w_fc2, 'bucket', scatter_dimension=0, tiled=True)  129 us
    unnamed x1, blocking collectives  75.2 us
    reduce_scatter x1, waiting for transfers between devices, body(): lax.psum_scatter(grad_table, 'bucket', scatter_dimension=1, tiled=True)  48.7 us
    unnamed x171, local copies, waits for them, and re-layouts  25.6 us
    dynamic_slice x24, local copies, waits for them, and re-layouts, body(): lax.map(attend, (query, key_rows, value_rows, same_crop))  24.4 us
  transfers between devices with their start and end apart: 14, of which 10 were waited for; matrix products, arithmetic and copies ran while one was open for 8% of the time, Pallas kernels for 0%

profile of v1, /device:TPU:0, one launch (start us, length us, event | category | flops | bytes accessed | tf_op | source)
XLA Modules:
  0.0 1107.1 jit_solution(8975024728227956439)
XLA Ops:
  9.2 8.4 all-to-all-start
  19.4 19.7 %all-to-all-done = bf16[16,24,1152]{2,1,0:T(8,128)(2,1)S(1)} async-done(((bf16[16,24,1152]{2,1,0:T(8,128)(2,1)}), bf16[16,24,1152]{2,1,0:T(8,128)(2,1)S(1)}, u32[]{:S(2)}, u32[]{:S(2)}) %all-to-all-start) | async-done | bytes 884768 | tf_op jit(solution)/shard_map/all_to_all | solution.py:82
  41.4 6.3 fusion.88
  60.5 4.6 fusion.86
  66.4 11.8 %all-gather.7.cloned.1.call-done = bf16[4,512,384]{1,2,0:T(8,128)(2,1)} async-done(((bf16[4,256,384]{1,2,0:T(8,128)(2,1)}), bf16[4,512,384]{1,2,0:T(8,128)(2,1)}) %all-gather.7.cloned.1.call-update) | async-done | bytes 1572880 | tf_op jit(solution)/shard_map/all_gather | solution.py:113
  78.2 19.8 %while.36 = (s32[]{:T(128)}, f32[4,256,6,64]{1,3,2,0:T(8,128)}, f32[4,6,256]{2,1,0:T(8,128)S(1)}, bf16[4,512,384]{1,2,0:T(8,128)(2,1)}, pred[4,256,512]{2,1,0:T(...) while((s32[]{:T(128)}, f32[4,256,6,64]{1,3,2,0:T(8,128)}, ...), condition=%wide.region_5.6_spmd, body=%wide.region_2.5_spmd.sunk | while | flops 210762240 | bytes 13490789 | solution.py:143
  108.1 3.5 fusion.47
  111.7 3.6 fusion.69
  115.3 7.4 convert_reduce_fusion
  137.3 23.6 %while.37 = (s32[]{:T(128)}, bf16[4,256,384]{2,1,0:T(8,128)(2,1)S(1)}, f32[4,6,256]{2,1,0:T(8,128)S(1)}, bf16[4,512,384]{1,2,0:T(8,128)(2,1)}, pred[4,256,512]{2...) while((s32[]{:T(128)}, ...), condition=%wide.region_13.14_spmd, body=%wide.region_11.13_spmd.sunk | while | flops 310835712 | bytes 20830336 | solution.py:238
  171.3 64.5 %while.38 = (s32[]{:T(128)}, bf16[4,256,384]{2,1,0:T(8,128)(2,1)}, bf16[4,256,384]{2,1,0:T(8,128)(2,1)}, bf16[4,512,384]{1,2,0:T(8,128)(2,1)}, pred[4,512,256]{2...) while((s32[]{:T(128)}, bf16[4,256,384]{2,1,0:T(8,128)(2,1)}, ...), condition=%wide.region_15.16_spmd, body=%wide.region_14.15_spmd.sunk | while | flops 410812416 | bytes 16132277 | solution.py:276
  239.2 4.6 convert_reduce_fusion.2
  264.8 5.1 fusion.110
  271.0 5.1 fusion.109
  282.2 4.4 convolution_bitcast_fusion
  290.2 109.6 %reduce-scatter.28.cloned.1.call-done = f32[384,24]{0,1:T(8,128)} async-done(((f32[384,384]{0,1:T(8,128)}), f32[384,24]{0,1:T(8,128)}) %reduce-scatter.28.cloned.1.call-update) | async-done | bytes 36880
  402.9 129.4 %reduce-scatter.20.cloned.1.call-done = f32[96,384]{1,0:T(8,128)} async-done(((f32[1536,384]{1,0:T(8,128)}), f32[96,384]{1,0:T(8,128)}) %reduce-scatter.20.cloned.1.call-update) | async-done | bytes 147472 | tf_op jit(solution)/shard_map/reduce_scatter | solution.py:197
  533.9 131.9 %reduce-scatter.18.cloned.1.call-done = f32[384,96]{0,1:T(8,128)} async-done(((f32[384,1536]{0,1:T(8,128)}), f32[384,96]{0,1:T(8,128)}) %reduce-scatter.18.cloned.1.call-update) | async-done | bytes 147472 | tf_op jit(solution)/shard_map/reduce_scatter | solution.py:195
  667.5 75.2 %all-reduce.9 = (f32[16,72]{1,0:T(8,128)S(1)}, bf16[768]{0:T(1024)(128)(2,1)S(1)}, bf16[384]{0:T(512)(128)(2,1)S(1)}, bf16[1536]{0:T(1024)(128)(2,1)S(1)}, bf16[...) all-reduce(f32[16,72]{1,0:T(8,128)S(1)} %reshape.267, ...), channel_id=5, replica_groups=mesh['bucket'=16,'seq'=2] {'bucket'}, use_global_device_ids=true, to_apply=%region_23.24.clone | all-reduce | flops 4608 | bytes 29952
  745.7 48.7 %reduce-scatter.16.cloned.1.call-done = f32[1000,24]{0,1:T(8,128)} async-done(((f32[1000,384]{0,1:T(8,128)}), f32[1000,24]{0,1:T(8,128)}) %reduce-scatter.16.cloned.1.call-update) | async-done | bytes 96016 | tf_op jit(solution)/shard_map/reduce_scatter | solution.py:325
  795.9 128.8 %reduce-scatter.26.cloned.1.call-done = f32[384,72]{0,1:T(8,128)} async-done(((f32[384,1152]{0,1:T(8,128)}), f32[384,72]{0,1:T(8,128)}) %reduce-scatter.26.cloned.1.call-update) | async-done | bytes 110608
  929.2 15.4 %all-reduce.17.cloned.1.call-done = (bf16[384,96]{0,1:T(8,128)(2,1)}, bf16[96,384]{1,0:T(8,128)(2,1)}) async-done(((bf16[384,96]{0,1:T(8,128)(2,1)}, bf16[96,384]{1,0:T(8,128)(2,1)}), (bf16[384,96]{0,1:T(8,128)(2,1)}, bf16[96,384]{1,0:T(8,128)(2,1)})) %all-reduce.17.cloned.1.call-update) | async-done | bytes 147472 | tf_op jit(solution)/shard_map/psum | solution.py:202
  947.7 20.3 %all-reduce.15.cloned.1.call-done = (bf16[1000,24]{0,1:T(8,128)(2,1)}, bf16[384,72]{0,1:T(8,128)(2,1)}, bf16[48]{0:T(256)(128)(2,1)}, bf16[384,24]{0,1:T(8,128)(...) async-done(((bf16[1000,24]{0,1:T(8,128)(2,1)}, bf16[384,72]{0,1:T(8,128)(2,1)}, bf16[48]{0:T(256)(128)(2,1)}, ...) | async-done | bytes 122176 | tf_op jit(solution)/shard_map/psum | solution.py:332
  978.0 122.4 %reduce-scatter.24.cloned.1.call-done = f32[24,1152]{1,0:T(8,128)} async-done(((f32[384,1152]{1,0:T(8,128)}), f32[24,1152]{1,0:T(8,128)}) %reduce-scatter.24.cloned.1.call-update) | async-done | bytes 110608
  (435 shorter events, 222.6 us)
Async XLA Ops:
  7.2 100.9 %copy-start = (bf16[384,1536]{1,0:T(8,128)(2,1)S(1)}, bf16[384,1536]{1,0:T(8,128)(2,1)}, u32[]{:S(2)}) copy-start(bf16[384,1536]{1,0:T(8,128)(2,1)} %param.43) | copy-start | bytes 3538948
  9.2 29.9 %all-to-all-start = ((bf16[16,24,1152]{2,1,0:T(8,128)(2,1)}), bf16[16,24,1152]{2,1,0:T(8,128)(2,1)S(1)}, u32[]{:S(2)}, u32[]{:S(2)}) async-start(bf16[16,24,1152]{2,1,0:T(8,128)(2,1)} %stack.2), calls=%async_computation | async-start | bytes 1769472 | tf_op jit(solution)/shard_map/all_to_all | solution.py:82
  17.7 48.8 %all-gather.5.cloned.1.call-start = ((), (), s32[]{:S(2)}) async-start(), calls=%async_computation.8 | async-start | bytes 2359296 | tf_op jit(solution)/shard_map/all_gather | solution.py:114
  17.8 42.6 %copy-start.40 = (s32[4,256]{1,0:T(4,128)}, s32[4,256]{1,0:T(4,128)S(1)}, u32[]{:S(2)}) copy-start(s32[4,256]{1,0:T(4,128)S(1)} %constant_dynamic-slice_fusion.10) | copy-start | bytes 12292
  18.1 29.6 %copy-start.38 = (f32[4,256]{1,0:T(4,128)}, f32[4,256]{1,0:T(4,128)S(1)}, u32[]{:S(2)}) copy-start(f32[4,256]{1,0:T(4,128)S(1)} %broadcast_multiply_fusion.2) | copy-start | bytes 12292
  18.6 29.1 %copy-start.44 = (f32[4,256]{1,0:T(4,128)}, f32[4,256]{1,0:T(4,128)S(1)}, u32[]{:S(2)}) copy-start(f32[4,256]{1,0:T(4,128)S(1)} %fusion.95) | copy-start | bytes 12292
  19.4 28.3 %copy-start.33 = (f32[4,8,384]{2,1,0:T(8,128)}, f32[4,8,384]{2,1,0:T(8,128)S(1)}, u32[]{:S(2)}) copy-start(f32[4,8,384]{2,1,0:T(8,128)S(1)} %convolution_add_fusion.3) | copy-start | bytes 147460
  56.2 22.0 %all-gather.7.cloned.1.call-start = ((), (), s32[]{:S(2)}) async-start(), calls=%async_computation.9 | async-start | bytes 2359296 | tf_op jit(solution)/shard_map/all_gather | solution.py:113
  59.1 107.5 %all-gather.11.cloned.1.call-start = ((), (), s32[]{:S(2)}) async-start(), calls=%async_computation.11 | async-start | bytes 2359296 | tf_op jit(solution)/shard_map/all_gather | solution.py:243
  60.0 69.4 %copy-start.48 = (f32[4,256]{1,0:T(4,128)}, f32[4,256]{1,0:T(4,128)S(1)}, u32[]{:S(2)}) copy-start(f32[4,256]{1,0:T(4,128)S(1)} %dynamic-slice_convert_fusion) | copy-start | bytes 12292
  104.2 23.0 %copy-start.2 = (f32[4,256,384]{2,1,0:T(8,128)}, f32[4,256,384]{2,1,0:T(8,128)S(1)}, u32[]{:S(2)}) copy-start(f32[4,256,384]{2,1,0:T(8,128)S(1)} %get-tuple-element.312) | copy-start | bytes 4718596
  135.8 33.6 %all-gather.9.cloned.1.call-start = ((), (), s32[]{:S(2)}) async-start(), calls=%async_computation.10 | async-start | bytes 2359296 | tf_op jit(solution)/shard_map/all_gather | solution.py:242
  137.0 139.2 %reduce-scatter.22.cloned.1.call-start = ((), (), s32[]{:S(2)}) async-start(), calls=%async_computation.15 | async-start | bytes 884736
  261.8 138.1 %reduce-scatter.28.cloned.1.call-start = ((), (), s32[]{:S(2)}) async-start(), calls=%async_computation.18 | async-start | bytes 626688
  264.5 267.8 %reduce-scatter.20.cloned.1.call-start = ((), (), s32[]{:S(2)}) async-start(), calls=%async_computation.14 | async-start | bytes 2506752 | tf_op jit(solution)/shard_map/reduce_scatter | solution.py:197
  269.9 395.8 %reduce-scatter.18.cloned.1.call-start = ((), (), s32[]{:S(2)}) async-start(), calls=%async_computation.13 | async-start | bytes 2506752 | tf_op jit(solution)/shard_map/reduce_scatter | solution.py:195
  276.2 518.2 %reduce-scatter.16.cloned.1.call-start = ((), (), s32[]{:S(2)}) async-start(), calls=%async_computation.12 | async-start | bytes 1671168 | tf_op jit(solution)/shard_map/reduce_scatter | solution.py:325
  282.1 642.5 %reduce-scatter.26.cloned.1.call-start = ((), (), s32[]{:S(2)}) async-start(), calls=%async_computation.17 | async-start | bytes 1880064
  286.6 658.0 %all-reduce.17.cloned.1.call-start = ((), (), s32[]{:S(2)}) async-start(), calls=%async_computation.20 | async-start | bytes 294912 | tf_op jit(solution)/shard_map/psum | solution.py:202
  289.1 378.4 %copy-start.59 = (f32[384]{0:T(512)S(1)}, f32[384]{0:T(512)}, u32[]{:S(2)}) copy-start(f32[384]{0:T(512)} %get-tuple-element.309) | copy-start | bytes 4612
  289.1 378.4 %copy-start.60 = (f32[1536]{0:T(1024)S(1)}, f32[1536]{0:T(1024)}, u32[]{:S(2)}) copy-start(f32[1536]{0:T(1024)} %get-tuple-element.345) | copy-start | bytes 18436
  667.3 300.7 %all-reduce.15.cloned.1.call-start = ((), (), s32[]{:S(2)}) async-start(), calls=%async_computation.19 | async-start | bytes 250880 | tf_op jit(solution)/shard_map/psum | solution.py:332
  926.2 174.2 %reduce-scatter.24.cloned.1.call-start = ((), (), s32[]{:S(2)}) async-start(), calls=%async_computation.16 | async-start | bytes 1880064
  926.3 174.2 %copy-start.1 = (bf16[384,1536]{1,0:T(8,128)(2,1)S(1)}, bf16[384,1536]{1,0:T(8,128)(2,1)}, u32[]{:S(2)}) copy-start(bf16[384,1536]{1,0:T(8,128)(2,1)} %param.43) | copy-start | bytes 3538948
  (75 other events, 290.6 us)
Sparse Core Ops, SparseCore 0:
  56.3 9.4 all-gather.4
  67.3 10.8 all-gather.6
  135.9 10.8 all-gather.10
  148.8 10.8 all-gather.8
  261.9 9.2 reduce-scatter.21
  276.4 123.4 reduce-scatter.27
  404.8 127.5 reduce-scatter.19
  538.0 127.6 reduce-scatter.17
  670.6 123.7 reduce-scatter.15
  799.1 125.5 reduce-scatter.25
  927.6 16.9 all-reduce.16
  948.4 19.5 all-reduce.14
  973.5 126.8 reduce-scatter.23
